TPU v7x, 32 devices: a whole 2x2x4 slice. The times are simulated.
32 devices in a mesh: cfg: 4 (over y, core), dom: 8 (over z, x).
Axes of the slice: x: 2, y: 2, z: 4, core: 2. Of those that a mesh axis runs over, the one named last changes fastest.
Arguments:
- features: bfloat16 [4, 12288, 512], P('cfg', 'dom'), may hold values from -6 to 6
- cotangent: bfloat16 [4, 12288, 512], P('cfg', 'dom'), may hold values from -6 to 6
- w_self: bfloat16 [512, 512], P('cfg'), may hold values from -0.25 to 0.25
- w_neigh: bfloat16 [512, 512], P('cfg'), may hold values from -0.25 to 0.25
- tiles: bfloat16 [64, 128, 128], P('dom'), may hold values from -0.3125 to 0.3125
- edge_peer: int32 [256, 1], P('dom'), may hold values from 0 to 7; in each aligned block of 32 rows (0 to 31, 32 to 63, ...) at most 8 rows name the same one
- edge_src: int32 [256], P('dom'), may hold values from 0 to 11
- edge_dst: int32 [256], P('dom'), may hold values from 0 to 11
- edge_tile: int32 [256], P('dom'), may hold values from 0 to 7
Outputs:
- hidden: bfloat16 [4, 12288, 512], P('cfg', 'dom')
- grad_self: float32 [512, 512], P('cfg')
- grad_neigh: float32 [512, 512], P('cfg')
Inputs may be any that keep to these rules, and one draw needn't show every extreme that they name: `edge_peer`: among the 32 edge blocks of one partition at most 8 have their destination on any one partition, and some destination partition takes exactly 8 of them.
All inputs are finite; a program needn't handle non-finite values.
Results may differ from a plain program's by a relative error of at most 0.0061.
Values may be sent and summed in bfloat16 or wider, within the bound.
No kernel may reach another device: no remote copies, remote signals or barrier semaphores. Data moves between devices by JAX's collectives and lax.ppermute only.
A program may use at most 128 MiB of HBM per device.

v0:
```python
import jax
import jax.numpy as jnp
from jax import lax
from jax.sharding import PartitionSpec as P


def head(pre):
    normed = pre * lax.rsqrt(jnp.mean(pre * pre, -1, keepdims=True) + 1e-05)
    return normed * jax.nn.sigmoid(normed)


def local(features, cotangent, w_self, w_neigh, tiles, edge_peer, edge_src, edge_dst, edge_tile):
    feats = features[0]
    rows, width = feats.shape
    tile = tiles.shape[1]
    blocks = rows // tile
    peers = lax.axis_size("dom")
    edges = edge_src.shape[0]
    per_peer = max(2, 2 * edges // peers)
    slots = peers * per_peer
    target = edge_peer[:, 0]
    peer_hot = (target[:, None] == jnp.arange(peers, dtype=jnp.int32)[None, :]).astype(jnp.int32)
    rank = jnp.sum((jnp.cumsum(peer_hot, 0) - 1) * peer_hot, 1)
    slot = target * per_peer + rank
    slot_hit = slot[:, None] == jnp.arange(slots, dtype=jnp.int32)[None, :]
    place = slot_hit.astype(jnp.bfloat16)
    labels = jnp.sum(jnp.where(slot_hit, (edge_dst + 1)[:, None], 0), 0)
    blocks_x = feats.reshape(blocks, tile, width)
    chosen = blocks_x[edge_src]
    chosen_tiles = tiles[edge_tile]
    partial_value = jnp.einsum(
        "etk,ekd->etd", chosen_tiles, chosen, preferred_element_type=jnp.float32
    ).astype(jnp.bfloat16)
    outgoing = jnp.einsum(
        "es,etd->std", place, partial_value, preferred_element_type=jnp.float32
    ).astype(jnp.bfloat16)
    got, got_labels = (
        lax.all_to_all(
            outgoing.reshape(peers, per_peer, tile, width),
            "dom",
            split_axis=0,
            concat_axis=0,
            tiled=True,
        ),
        lax.all_to_all(
            labels.reshape(peers, per_peer), "dom", split_axis=0, concat_axis=0, tiled=True
        ),
    )
    arrived = got.reshape(slots, tile, width)
    owner_hot = (
        got_labels.reshape(slots)[:, None] - 1 == jnp.arange(blocks, dtype=jnp.int32)[None, :]
    ).astype(jnp.bfloat16)
    aggregate = (
        jnp.einsum("sb,std->btd", owner_hot, arrived, preferred_element_type=jnp.float32)
        .reshape(rows, width)
        .astype(jnp.bfloat16)
    )
    total = jnp.dot(
        feats, lax.all_gather(w_self, "cfg", axis=0, tiled=True), preferred_element_type=jnp.float32
    )
    pre = total + jnp.dot(
        aggregate,
        lax.all_gather(w_neigh, "cfg", axis=0, tiled=True),
        preferred_element_type=jnp.float32,
    )
    out, pullback = jax.vjp(head, pre)
    grad_pre = pullback(cotangent[0].astype(jnp.float32))[0].astype(jnp.bfloat16)
    term_s = lax.dot_general(
        feats, grad_pre, (((0,), (0,)), ((), ())), preferred_element_type=jnp.float32
    )
    term_n = lax.dot_general(
        aggregate, grad_pre, (((0,), (0,)), ((), ())), preferred_element_type=jnp.float32
    )
    total_s, total_n = lax.psum((term_s, term_n), "dom")
    share_s, share_n = (
        lax.psum_scatter(total_s, "cfg", scatter_dimension=0, tiled=True),
        lax.psum_scatter(total_n, "cfg", scatter_dimension=0, tiled=True),
    )
    factor = float(lax.axis_size("cfg") * peers * rows) ** (-0.5)
    return (out.astype(jnp.bfloat16)[None], share_s * factor, share_n * factor)


def solution(mesh):
    placed = (
        P("cfg", "dom", None),
        P("cfg", "dom", None),
        P("cfg", None),
        P("cfg", None),
        P("dom", None, None),
        P("dom", None),
        P("dom"),
        P("dom"),
        P("dom"),
    )
    return jax.shard_map(
        local,
        mesh=mesh,
        in_specs=placed,
        out_specs=(P("cfg", "dom", None), P("cfg", None), P("cfg", None)),
        check_vma=False,
    )
```

profile of v0, /device:TPU:0, one launch (start us, length us, event | category | flops | bytes accessed | tf_op | source)
XLA Modules:
  0.0 381.3 jit_solution(4688032224034469824)
XLA Ops:
  7.2 0.8 fusion.19
  8.1 0.8 select_reduce_fusion.1
  8.9 0.7 fusion.26
  10.3 0.7 all_to_all.9
  11.0 7.3 %all-to-all-start = ((s32[8,1,8]{2,1,0:T(1,128)}), s32[8,1,8]{2,1,0:T(1,128)S(1)}, u32[]{:S(2)}, u32[]{:S(2)}) async-start(s32[8,1,8]{2,1,0:T(1,128)} %bitcast.4), calls=%async_computation | async-start | bytes 8192 | tf_op jit(solution)/shard_map/all_to_all | solution.py:45
  19.6 2.7 gather_fusion.1
  22.4 0.7 gather_fusion
  23.1 3.4 convolution_convert_fusion
  26.6 6.5 %convert_bitcast_fusion = bf16[8,8,128,512]{3,1,0,2:T(8,128)(2,1)} fusion(bf16[32,128,512]{2,1,0:T(8,128)(2,1)S(1)} %convolution_convert_fusion, s32[32]{0:T(128)S(1)} %fusion.26), kind=kOutput, calls=%fused_computation.5 | convolution fusion | flops 272631808 | bytes 12583040 | tf_op jit(solution)/shard_map/es,etd->std/dot_general | solution.py:34
  33.1 7.4 %copy.25 = bf16[8,8,128,512]{3,1,2,0:T(8,128)(2,1)} copy(bf16[8,8,128,512]{3,1,0,2:T(8,128)(2,1)} %convert_bitcast_fusion) | data formatting | bytes 16777216 | tf_op jit(solution)/shard_map/reshape | solution.py:39
  40.5 6.0 %all-to-all-start.1 = ((bf16[8,8,128,512]{3,1,2,0:T(8,128)(2,1)}), bf16[8,8,128,512]{3,1,2,0:T(8,128)(2,1)}, u32[]{:S(2)}, u32[]{:S(2)}) async-start(bf16[8,8,128,512]{3,1,2,0:T(8,128)(2,1)} %copy.25), calls=%async_computation.1 | async-start | bytes 16777216 | tf_op jit(solution)/shard_map/all_to_all | solution.py:38
  46.6 1.8 copy.28
  48.4 7.2 %all_gather.6 = bf16[512,512]{1,0:T(8,128)(2,1)S(1)} all-gather(bf16[128,512]{1,0:T(8,128)(2,1)S(1)} %copy-done.6), channel_id=1, replica_groups=mesh['cfg'=4,'dom'=8] {'cfg'}, dimensions={0}, use_global_device_ids=true | all-gather | bytes 655360 | tf_op jit(solution)/shard_map/all_gather | solution.py:59
  55.6 7.9 %all_gather.7 = bf16[512,512]{1,0:T(8,128)(2,1)} all-gather(bf16[128,512]{1,0:T(8,128)(2,1)S(1)} %copy-done.7), channel_id=1, replica_groups=mesh['cfg'=4,'dom'=8] {'cfg'}, dimensions={0}, use_global_device_ids=true | all-gather | bytes 655360 | tf_op jit(solution)/shard_map/all_gather | solution.py:63
  63.5 2.7 fusion.12
  66.3 162.9 %all-to-all-done.1 = bf16[8,8,128,512]{3,1,2,0:T(8,128)(2,1)} async-done(((bf16[8,8,128,512]{3,1,2,0:T(8,128)(2,1)}), bf16[8,8,128,512]{3,1,2,0:T(8,128)(2,1)}, u32[]{:S(2)}, u32[]{:S(2)}) %all-to-all-start.1) | async-done | bytes 8388640 | tf_op jit(solution)/shard_map/all_to_all | solution.py:38
  229.1 4.6 %fusion.7 = bf16[12,128,512]{2,0,1:T(8,128)(2,1)S(1)} fusion(bf16[8,8,128,512]{3,1,2,0:T(8,128)(2,1)} %all-to-all-done.1, s32[64]{0:T(128)S(1)} %sub.15), kind=kOutput, calls=%fused_computation.20 | convolution fusion | flops 101450496 | bytes 9961728 | tf_op jit(solution)/shard_map/sb,std->btd/dot_general | solution.py:54
  233.7 0.9 copy.27
  234.6 1.0 copy-done.1
  235.7 1.1 multiply_reduce_fusion.1
  236.8 1.5 multiply_reduce_fusion
  238.3 2.9 fusion.6
  241.2 1.2 copy-done.5
  242.3 1.9 fusion.27
  244.4 3.5 fusion.15
  247.9 20.4 %reduce-scatter.5.cloned.1.call-done = f32[128,512]{0,1:T(8,128)} async-done(((f32[512,512]{0,1:T(8,128)}), f32[128,512]{0,1:T(8,128)}) %reduce-scatter.5.cloned.1.call-update) | async-done | bytes 262160 | tf_op jit(solution)/shard_map/reduce_scatter | solution.py:77
  268.4 27.3 %reduce-scatter.3.cloned.1.call-done = f32[128,512]{0,1:T(8,128)} async-done(((f32[512,512]{0,1:T(8,128)}), f32[128,512]{0,1:T(8,128)}) %reduce-scatter.3.cloned.1.call-update) | async-done | bytes 262160 | tf_op jit(solution)/shard_map/reduce_scatter | solution.py:76
  295.7 1.6 copy.30
  297.3 74.7 %all-reduce.3.cloned.1.call-done = (f32[128,512]{0,1:T(8,128)}, f32[128,512]{0,1:T(8,128)}) async-done(((f32[128,512]{0,1:T(8,128)}, f32[128,512]{0,1:T(8,128)}), (f32[128,512]{0,1:T(8,128)}, f32[128,512]{0,1:T(8,128)})) %all-reduce.3.cloned.1.call-update) | async-done | bytes 524304 | tf_op jit(solution)/shard_map/psum | solution.py:74
  372.0 1.1 broadcast_multiply_fusion
  373.1 0.8 copy.31
  373.9 0.8 copy.32
  (32 shorter events, 2.6 us)
Async XLA Ops:
  7.2 12.5 %copy-start = (bf16[1,1536,512]{2,1,0:T(8,128)(2,1)S(1)}, bf16[1,1536,512]{2,1,0:T(8,128)(2,1)}, u32[]{:S(2)}) copy-start(bf16[1,1536,512]{2,1,0:T(8,128)(2,1)} %param.9) | copy-start | bytes 4718596
  11.0 29.5 %all-to-all-start = ((s32[8,1,8]{2,1,0:T(1,128)}), s32[8,1,8]{2,1,0:T(1,128)S(1)}, u32[]{:S(2)}, u32[]{:S(2)}) async-start(s32[8,1,8]{2,1,0:T(1,128)} %bitcast.4), calls=%async_computation | async-start | bytes 8192 | tf_op jit(solution)/shard_map/all_to_all | solution.py:45
  19.6 2.8 copy-start.3
  40.5 188.6 %all-to-all-start.1 = ((bf16[8,8,128,512]{3,1,2,0:T(8,128)(2,1)}), bf16[8,8,128,512]{3,1,2,0:T(8,128)(2,1)}, u32[]{:S(2)}, u32[]{:S(2)}) async-start(bf16[8,8,128,512]{3,1,2,0:T(8,128)(2,1)} %copy.25), calls=%async_computation.1 | async-start | bytes 16777216 | tf_op jit(solution)/shard_map/all_to_all | solution.py:38
  46.5 1.8 copy-start.6
  46.5 9.0 %copy-start.7 = (bf16[128,512]{1,0:T(8,128)(2,1)S(1)}, bf16[128,512]{1,0:T(8,128)(2,1)}, u32[]{:S(2)}) copy-start(bf16[128,512]{1,0:T(8,128)(2,1)} %param.12) | copy-start | bytes 393220
  46.5 221.8 %reduce-scatter.5.cloned.1.call-start = ((), (), s32[]{:S(2)}) async-start(), calls=%async_computation.5 | async-start | bytes 1310720 | tf_op jit(solution)/shard_map/reduce_scatter | solution.py:77
  233.7 1.9 copy-start.1
  233.7 2.0 copy-start.4
  241.2 1.2 copy-start.5
  244.3 51.4 %copy-start.2 = (bf16[1,1536,512]{1,2,0:T(8,128)(2,1)S(1)}, bf16[1,1536,512]{1,2,0:T(8,128)(2,1)}, u32[]{:S(2)}) copy-start(bf16[1,1536,512]{1,2,0:T(8,128)(2,1)} %get-tuple-element.15) | copy-start | bytes 4718596
  244.3 51.4 %reduce-scatter.3.cloned.1.call-start = ((), (), s32[]{:S(2)}) async-start(), calls=%async_computation.4 | async-start | bytes 1310720 | tf_op jit(solution)/shard_map/reduce_scatter | solution.py:76
  247.9 124.1 %all-reduce.3.cloned.1.call-start = ((), (), s32[]{:S(2)}) async-start(), calls=%async_computation.6 | async-start | bytes 1048576 | tf_op jit(solution)/shard_map/psum | solution.py:74
Sparse Core Ops, SparseCore 0:
  244.4 23.8 reduce-scatter.4
  270.9 24.7 reduce-scatter.2
  299.2 72.7 all-reduce.2
where the time goes:
time: 382 us; the launch traced here: 381 us
  waiting for transfers between devices  285 us (75%)
  matrix products  23.8 us (6%)
  local copies, waits for them, and re-layouts  19.8 us (5%)
  blocking collectives  15.1 us (4%)
  between operations  13.9 us (4%)
  starting transfers between devices  13.4 us (4%)
  other arithmetic  9.93 us (3%)
    all_to_all x1, waiting for transfers between devices, local(): lax.all_to_all(outgoing.reshape(peers, per_peer, tile, width), 'dom', spl...  163 us
    psum x1, waiting for transfers between devices, local(): total_s, total_n = lax.psum((term_s, term_n), 'dom')  74.7 us
    reduce_scatter x1, waiting for transfers between devices, local(): lax.psum_scatter(total_s, 'cfg', scatter_dimension=0, tiled=True)  27.3 us
    reduce_scatter x1, waiting for transfers between devices, local(): lax.psum_scatter(total_n, 'cfg', scatter_dimension=0, tiled=True)  20.4 us
    all_gather x1, blocking collectives, local(): lax.all_gather(w_neigh, 'cfg', axis=0, tiled=True)  7.89 us
  transfers between devices with their start and end apart: 5, of which 4 were waited for; matrix products, arithmetic and copies ran while one was open for 8% of the time, Pallas kernels for 0%

commit v1 on v0

--- a/solution.py
+++ b/solution.py
@@ -1,7 +1,29 @@
+import functools
 import jax
 import jax.numpy as jnp
 from jax import lax
 from jax.sharding import PartitionSpec as P
+
+
+def fit_bars(array_in, peer_axis):
+    w2 = lax.psum(1, peer_axis)
+    now, base_arr = (w2, lax.axis_index(peer_axis))
+    arr_now = list(array_in.shape)
+    y2 = array_in.shape[0] // now
+    arr_now[0] = y2
+    everything = arr_now[0]
+    arr_now[0] = everything * now
+    y = jnp.zeros(arr_now, array_in.dtype)
+    for no in range(now):
+        known = lax.dynamic_slice_in_dim(array_in, (base_arr ^ no) * y2, y2, axis=0)
+        if no:
+            back = tuple(((j, j ^ no) for j in range(now)))
+            known = lax.ppermute(known, peer_axis, back)
+        y = lax.dynamic_update_slice_in_dim(y, known, (base_arr ^ no) * everything, axis=0)
+    return y
+
+
+_part_loads = functools.partial(fit_bars, peer_axis="dom")
 
 
 def head(pre):
@@ -35,13 +57,7 @@
         "es,etd->std", place, partial_value, preferred_element_type=jnp.float32
     ).astype(jnp.bfloat16)
     got, got_labels = (
-        lax.all_to_all(
-            outgoing.reshape(peers, per_peer, tile, width),
-            "dom",
-            split_axis=0,
-            concat_axis=0,
-            tiled=True,
-        ),
+        _part_loads(outgoing.reshape(peers, per_peer, tile, width)),
         lax.all_to_all(
             labels.reshape(peers, per_peer), "dom", split_axis=0, concat_axis=0, tiled=True
         ),

time: 382 us -> 373 us (0.976)
  waiting for transfers between devices: 285 us -> 258 us
  local copies, waits for them, and re-layouts: 19.8 us -> 36.1 us
  starting transfers between devices: 13.4 us -> 18.6 us
    all_to_all x1 -> x0, waiting for transfers between devices: 163 us -> none  [local(): lax.all_to_all(outgoing.reshape(peers, per_peer, tile, width), 'dom', spl...]
    all_to_all x1, waiting for transfers between devices: 0.01 us -> 62.1 us  [local(): lax.all_to_all(labels.reshape(peers, per_peer), 'dom', split_axis=0, conc...]
    ppermute x0 -> x7, waiting for transfers between devices: none -> 44.7 us  [fit_bars(): known = lax.ppermute(known, peer_axis, back)]
    reduce_scatter x1, waiting for transfers between devices: 20.4 us -> 49.6 us  [local(): lax.psum_scatter(total_n, 'cfg', scatter_dimension=0, tiled=True)]
    dynamic_update_slice x0 -> x7, local copies, waits for them, and re-layouts: none -> 16.4 us  [fit_bars(): lax.dynamic_update_slice_in_dim(y, known, (base_arr ^ no) * everything, a...]
    ppermute x0 -> x7, starting transfers between devices: none -> 13.6 us  [fit_bars(): known = lax.ppermute(known, peer_axis, back)]
    reshape x1 -> x0, local copies, waits for them, and re-layouts: 7.41 us -> none  [local(): outgoing.reshape(peers, per_peer, tile, width)]
    all_to_all x1 -> x0, starting transfers between devices: 6 us -> none  [local(): lax.all_to_all(outgoing.reshape(peers, per_peer, tile, width), 'dom', spl...]
  transfers between devices with their start and end apart: 5 -> 11, of which waited for: 4 -> 6; matrix products, arithmetic and copies ran while one was open for 8% -> 6% of each run, Pallas kernels for 0% -> 0%
where the time goes in v1:
time: 373 us; the launch traced here: 372 us
  waiting for transfers between devices  258 us (69%)
  local copies, waits for them, and re-layouts  36.1 us (10%)
  matrix products  20.6 us (6%)
  starting transfers between devices  18.6 us (5%)
  blocking collectives  15 us (4%)
  between operations  14 us (4%)
  other arithmetic  9.5 us (3%)
    psum x1, waiting for transfers between devices, local(): total_s, total_n = lax.psum((term_s, term_n), 'dom')  74.7 us
    all_to_all x1, waiting for transfers between devices, local(): lax.all_to_all(labels.reshape(peers, per_peer), 'dom', split_axis=0, conc...  62.1 us
    reduce_scatter x1, waiting for transfers between devices, local(): lax.psum_scatter(total_n, 'cfg', scatter_dimension=0, tiled=True)  49.6 us
    ppermute x7, waiting for transfers between devices, fit_bars(): known = lax.ppermute(known, peer_axis, back)  44.7 us
    reduce_scatter x1, waiting for transfers between devices, local(): lax.psum_scatter(total_s, 'cfg', scatter_dimension=0, tiled=True)  27.3 us
    dynamic_update_slice x7, local copies, waits for them, and re-layouts, fit_bars(): lax.dynamic_update_slice_in_dim(y, known, (base_arr ^ no) * everything, a...  16.4 us
    ppermute x7, starting transfers between devices, fit_bars(): known = lax.ppermute(known, peer_axis, back)  13.6 us
    unnamed x24, local copies, waits for them, and re-layouts  10.5 us
  transfers between devices with their start and end apart: 11, of which 6 were waited for; matrix products, arithmetic and copies ran while one was open for 6% of the time, Pallas kernels for 0%

profile of v1, /device:TPU:0, one launch (start us, length us, event | category | flops | bytes accessed | tf_op | source)
XLA Modules:
  0.0 372.3 jit_solution(13885733200684707960)
XLA Ops:
  10.4 2.8 gather_fusion.1
  13.9 3.4 convolution_convert_fusion
  17.3 3.3 convert_bitcast_fusion
  21.7 3.0 constant_dynamic-slice_fusion.6
  24.7 3.2 copy-done.1
  27.9 3.0 collective-permute-start
  30.9 1.6 collective-permute-start.1
  32.5 3.0 collective-permute-start.3
  37.5 4.9 %all-to-all-start = ((s32[8,1,8]{2,1,0:T(1,128)}), s32[8,1,8]{2,1,0:T(1,128)S(1)}, u32[]{:S(2)}, u32[]{:S(2)}) async-start(s32[8,1,8]{2,1,0:T(1,128)} %bitcast.4), calls=%async_computation | async-start | bytes 8192 | tf_op jit(solution)/shard_map/all_to_all | solution.py:61
  42.5 7.2 %all_gather.6 = bf16[512,512]{1,0:T(8,128)(2,1)S(1)} all-gather(bf16[128,512]{1,0:T(8,128)(2,1)S(1)} %copy-done.7), channel_id=1, replica_groups=mesh['cfg'=4,'dom'=8] {'cfg'}, dimensions={0}, use_global_device_ids=true | all-gather | bytes 655360 | tf_op jit(solution)/shard_map/all_gather | solution.py:75
  49.7 4.7 %collective-permute-done = bf16[1,8,128,512]{3,1,0,2:T(8,128)(2,1)} collective-permute-done((bf16[1,8,128,512]{3,1,0,2:T(8,128)(2,1)}, bf16[1,8,128,512]{3,1,0,2:T(8,128)(2,1)}, u32[]{:S(2)}, u32[]{:S(2)}) %collective-permute-start) | collective-permute-done | bytes 1048608 | tf_op jit(solution)/shard_map/ppermute | solution.py:21
  54.4 3.9 %collective-permute-start.5 = (bf16[1,8,128,512]{3,1,0,2:T(8,128)(2,1)}, bf16[1,8,128,512]{3,1,0,2:T(8,128)(2,1)}, u32[]{:S(2)}, u32[]{:S(2)}) collective-permute-start(bf16[1,8,128,512]{3,1,0,2:T(8,128)(2,1)} %get-tuple-element.15), channel_id=1, source_target_pairs={{0,6},{1,7},{2,4},{3,5},{4,2},{5,3},{6,0},{7,1},{8,14},{9,15},{10,... | collective-permute-start | bytes 3145736 | tf_op jit(solution)/shard_map/ppermute | solution.py:21
  58.2 2.8 fusion.11
  61.0 40.0 %collective-permute-done.1 = bf16[1,8,128,512]{3,1,0,2:T(8,128)(2,1)} collective-permute-done((bf16[1,8,128,512]{3,1,0,2:T(8,128)(2,1)S(1)}, bf16[1,8,128,512]{3,1,0,2:T(8,128)(2,1)}, u32[]{:S(2)}, u32[]{:S(2)}) %collective-permute-start.1) | collective-permute-done | bytes 1048608 | tf_op jit(solution)/shard_map/ppermute | solution.py:21
  101.9 7.8 %all_gather.7 = bf16[512,512]{1,0:T(8,128)(2,1)} all-gather(bf16[128,512]{1,0:T(8,128)(2,1)S(1)} %copy-done.8), channel_id=1, replica_groups=mesh['cfg'=4,'dom'=8] {'cfg'}, dimensions={0}, use_global_device_ids=true | all-gather | bytes 655360 | tf_op jit(solution)/shard_map/all_gather | solution.py:79
  109.7 1.7 copy.26
  111.4 62.1 %all-to-all-done = s32[8,1,8]{2,1,0:T(1,128)S(1)} async-done(((s32[8,1,8]{2,1,0:T(1,128)}), s32[8,1,8]{2,1,0:T(1,128)S(1)}, u32[]{:S(2)}, u32[]{:S(2)}) %all-to-all-start) | async-done | bytes 288 | tf_op jit(solution)/shard_map/all_to_all | solution.py:61
  173.6 2.4 constant_dynamic-update-slice_fusion.5
  175.9 2.3 constant_dynamic-update-slice_fusion.4
  178.3 2.4 constant_dynamic-update-slice_fusion.3
  180.6 2.4 constant_dynamic-update-slice_fusion.2
  183.0 2.3 constant_dynamic-update-slice_fusion.1
  185.3 2.4 constant_dynamic-update-slice_fusion
  187.7 2.3 constant_dynamic-update-slice_fusion.6
  190.0 4.6 %fusion.6 = bf16[12,128,512]{2,0,1:T(8,128)(2,1)S(1)} fusion(bf16[8,8,128,512]{3,1,0,2:T(8,128)(2,1)} %constant_dynamic-update-slice_fusion.6, s32[64]{0:T(128)S(1)} %sub.15), kind=kOutput, calls=%fused_computation.19 | convolution fusion | flops 101450496 | bytes 9961728 | tf_op jit(solution)/shard_map/sb,std->btd/dot_general | solution.py:70
  199.3 2.9 fusion.5
  203.3 2.0 fusion.26
  205.3 3.5 fusion.14
  208.8 49.6 %reduce-scatter.5.cloned.1.call-done = f32[128,512]{0,1:T(8,128)} async-done(((f32[512,512]{0,1:T(8,128)}), f32[128,512]{0,1:T(8,128)}) %reduce-scatter.5.cloned.1.call-update) | async-done | bytes 262160 | tf_op jit(solution)/shard_map/reduce_scatter | solution.py:93
  258.5 27.3 %reduce-scatter.3.cloned.1.call-done = f32[128,512]{0,1:T(8,128)} async-done(((f32[512,512]{0,1:T(8,128)}), f32[128,512]{0,1:T(8,128)}) %reduce-scatter.3.cloned.1.call-update) | async-done | bytes 262160 | tf_op jit(solution)/shard_map/reduce_scatter | solution.py:92
  285.8 1.6 copy.28
  287.4 74.7 %all-reduce.3.cloned.1.call-done = (f32[128,512]{0,1:T(8,128)}, f32[128,512]{0,1:T(8,128)}) async-done(((f32[128,512]{0,1:T(8,128)}, f32[128,512]{0,1:T(8,128)}), (f32[128,512]{0,1:T(8,128)}, f32[128,512]{0,1:T(8,128)})) %all-reduce.3.cloned.1.call-update) | async-done | bytes 524304 | tf_op jit(solution)/shard_map/psum | solution.py:90
  (56 shorter events, 17.5 us)
Async XLA Ops:
  7.2 3.2 copy-start
  10.3 2.8 copy-start.4
  21.7 15.1 %copy-start.9 = (s32[32]{0:T(128)S(1)}, s32[32]{0:T(128)}, u32[]{:S(2)}) copy-start(s32[32]{0:T(128)} %param.16) | copy-start | bytes 388
  21.7 20.8 %copy-start.7 = (bf16[128,512]{1,0:T(8,128)(2,1)S(1)}, bf16[128,512]{1,0:T(8,128)(2,1)}, u32[]{:S(2)}) copy-start(bf16[128,512]{1,0:T(8,128)(2,1)} %param.11) | copy-start | bytes 393220
  24.7 3.2 copy-start.1
  27.9 26.4 %collective-permute-start = (bf16[1,8,128,512]{3,1,0,2:T(8,128)(2,1)}, bf16[1,8,128,512]{3,1,0,2:T(8,128)(2,1)}, u32[]{:S(2)}, u32[]{:S(2)}) collective-permute-start(bf16[1,8,128,512]{3,1,0,2:T(8,128)(2,1)} %get-tuple-element.20), channel_id=1, source_target_pairs={{0,1},{1,0},{2,3},{3,2},{4,5},{5,4},{6,7},{7,6},{8,9},{9,8},{10,11... | collective-permute-start | bytes 3145736 | tf_op jit(solution)/shard_map/ppermute | solution.py:21
  30.9 70.1 %collective-permute-start.1 = (bf16[1,8,128,512]{3,1,0,2:T(8,128)(2,1)S(1)}, bf16[1,8,128,512]{3,1,0,2:T(8,128)(2,1)}, u32[]{:S(2)}, u32[]{:S(2)}) collective-permute-start(bf16[1,8,128,512]{3,1,0,2:T(8,128)(2,1)S(1)} %get-tuple-element.19), channel_id=1, source_target_pairs={{0,2},{1,3},{2,0},{3,1},{4,6},{5,7},{6,4},{7,5},{8,10},{9,11},{10,... | collective-permute-start | bytes 3145736 | tf_op jit(solution)/shard_map/ppermute | solution.py:21
  32.5 145.8 %collective-permute-start.2 = (bf16[1,8,128,512]{3,1,0,2:T(8,128)(2,1)}, bf16[1,8,128,512]{3,1,0,2:T(8,128)(2,1)}, u32[]{:S(2)}, u32[]{:S(2)}) collective-permute-start(bf16[1,8,128,512]{3,1,0,2:T(8,128)(2,1)} %get-tuple-element.18), channel_id=1, source_target_pairs={{0,3},{1,2},{2,1},{3,0},{4,7},{5,6},{6,5},{7,4},{8,11},{9,10},{10,... | collective-permute-start | bytes 3145736 | tf_op jit(solution)/shard_map/ppermute | solution.py:21
  32.5 148.2 %collective-permute-start.3 = (bf16[1,8,128,512]{3,1,0,2:T(8,128)(2,1)}, bf16[1,8,128,512]{3,1,0,2:T(8,128)(2,1)}, u32[]{:S(2)}, u32[]{:S(2)}) collective-permute-start(bf16[1,8,128,512]{3,1,0,2:T(8,128)(2,1)} %get-tuple-element.17), channel_id=1, source_target_pairs={{0,4},{1,5},{2,6},{3,7},{4,0},{5,1},{6,2},{7,3},{8,12},{9,13},{10,... | collective-permute-start | bytes 3145736 | tf_op jit(solution)/shard_map/ppermute | solution.py:21
  35.5 147.5 %collective-permute-start.4 = (bf16[1,8,128,512]{3,1,0,2:T(8,128)(2,1)}, bf16[1,8,128,512]{3,1,0,2:T(8,128)(2,1)}, u32[]{:S(2)}, u32[]{:S(2)}) collective-permute-start(bf16[1,8,128,512]{3,1,0,2:T(8,128)(2,1)} %get-tuple-element.16), channel_id=1, source_target_pairs={{0,5},{1,4},{2,7},{3,6},{4,1},{5,0},{6,3},{7,2},{8,13},{9,12},{10,... | collective-permute-start | bytes 3145736 | tf_op jit(solution)/shard_map/ppermute | solution.py:21
  37.5 135.9 %all-to-all-start = ((s32[8,1,8]{2,1,0:T(1,128)}), s32[8,1,8]{2,1,0:T(1,128)S(1)}, u32[]{:S(2)}, u32[]{:S(2)}) async-start(s32[8,1,8]{2,1,0:T(1,128)} %bitcast.4), calls=%async_computation | async-start | bytes 8192 | tf_op jit(solution)/shard_map/all_to_all | solution.py:61
  42.4 216.1 %reduce-scatter.5.cloned.1.call-start = ((), (), s32[]{:S(2)}) async-start(), calls=%async_computation.4 | async-start | bytes 1310720 | tf_op jit(solution)/shard_map/reduce_scatter | solution.py:93
  54.4 47.5 %copy-start.8 = (bf16[128,512]{1,0:T(8,128)(2,1)S(1)}, bf16[128,512]{1,0:T(8,128)(2,1)}, u32[]{:S(2)}) copy-start(bf16[128,512]{1,0:T(8,128)(2,1)} %param.12) | copy-start | bytes 393220
  54.4 130.9 %collective-permute-start.5 = (bf16[1,8,128,512]{3,1,0,2:T(8,128)(2,1)}, bf16[1,8,128,512]{3,1,0,2:T(8,128)(2,1)}, u32[]{:S(2)}, u32[]{:S(2)}) collective-permute-start(bf16[1,8,128,512]{3,1,0,2:T(8,128)(2,1)} %get-tuple-element.15), channel_id=1, source_target_pairs={{0,6},{1,7},{2,4},{3,5},{4,2},{5,3},{6,0},{7,1},{8,14},{9,15},{10,... | collective-permute-start | bytes 3145736 | tf_op jit(solution)/shard_map/ppermute | solution.py:21
  101.0 86.7 %collective-permute-start.6 = (bf16[1,8,128,512]{3,1,0,2:T(8,128)(2,1)}, bf16[1,8,128,512]{3,1,0,2:T(8,128)(2,1)}, u32[]{:S(2)}, u32[]{:S(2)}) collective-permute-start(bf16[1,8,128,512]{3,1,0,2:T(8,128)(2,1)} %get-tuple-element.14), channel_id=1, source_target_pairs={{0,7},{1,6},{2,5},{3,4},{4,3},{5,2},{6,1},{7,0},{8,15},{9,14},{10,... | collective-permute-start | bytes 3145736 | tf_op jit(solution)/shard_map/ppermute | solution.py:21
  194.6 1.9 copy-start.2
  194.6 2.0 copy-start.5
  202.1 1.1 copy-start.6
  205.2 80.6 %copy-start.3 = (bf16[1,1536,512]{1,2,0:T(8,128)(2,1)S(1)}, bf16[1,1536,512]{1,2,0:T(8,128)(2,1)}, u32[]{:S(2)}) copy-start(bf16[1,1536,512]{1,2,0:T(8,128)(2,1)} %get-tuple-element.23) | copy-start | bytes 4718596
  205.2 80.6 %reduce-scatter.3.cloned.1.call-start = ((), (), s32[]{:S(2)}) async-start(), calls=%async_computation.3 | async-start | bytes 1310720 | tf_op jit(solution)/shard_map/reduce_scatter | solution.py:92
  208.8 153.4 %all-reduce.3.cloned.1.call-start = ((), (), s32[]{:S(2)}) async-start(), calls=%async_computation.5 | async-start | bytes 1048576 | tf_op jit(solution)/shard_map/psum | solution.py:90
Sparse Core Ops, SparseCore 0:
  205.4 53.0 reduce-scatter.4
  261.0 24.7 reduce-scatter.2
  289.3 72.8 all-reduce.2
